TPU v7x, 128 devices: a whole 4x4x4 slice. The times are simulated.
128 devices in a mesh: dp: 32 (over z_lo, x, y), tensor: 4 (over z_hi, core).
Axes of the slice: x: 4, y: 4, z: 4 (z_hi: 2, z_lo: 2; z = z_hi * 2 + z_lo), core: 2. Of those that a mesh axis runs over, the one named last changes fastest.
Arguments:
- hidden: bfloat16 [64, 512, 5120], P('dp'), may hold values from -5 to 5
- query_projection_matrix: bfloat16 [5120, 2560], P('dp', 'tensor'), may hold values from -0.5 to 0.5
- key_projection_matrix: bfloat16 [5120, 2560], P('dp', 'tensor'), may hold values from -0.5 to 0.5
- value_projection_matrix: bfloat16 [5120, 2560], P('dp', 'tensor'), may hold values from -0.078125 to 0.078125
- adapter_down_maps: bfloat16 [2, 8, 5120], replicated, may hold values from -0.078125 to 0.078125
- adapter_up_maps: bfloat16 [2, 8, 2560], P(None, None, 'tensor'), may hold values from -1 to 1
- cotangent: bfloat16 [64, 512, 2560], P('dp', None, 'tensor'), may hold values from -6 to 6
- lengths: int32 [64], P('dp'), may hold values from 1 to 512, 16640 in all
- random_signs_down: bfloat16 [2, 8, 5120, 4096], P(None, None, ('dp', 'tensor')), may hold values from -4 to 4
- random_signs_up: bfloat16 [2, 8, 20, 128, 4096], P(None, None, 'tensor', 'dp'), may hold values from -4 to 4
Outputs:
- features: float32 [64, 4096], P('dp', 'tensor')
Inputs may be any that keep to these rules, and one draw needn't show every extreme that they name: `lengths`: positions at or beyond an example's length are padding.
All inputs are finite; a program needn't handle non-finite values. No bound on the sum of `lengths` on one device may be relied on, other than what follows from the above.
Results may differ from a plain program's by a relative error of at most 0.025.
Values may be sent and summed in bfloat16 or wider, within the bound.
A program may use at most 128 MiB of HBM per device.

v0:
```python
import jax
import jax.numpy as jnp
from jax import lax
from jax.sharding import PartitionSpec as P

HEAD_DIM = 128
ADAPTER_RANK = 8
FEAT = 4096
adapter_scale = 2.0
rope_base = 10000.0
norm_eps = 1e-05
masked_score = -1e30


def rope_tables(seq_len, head_width):
    half_width = head_width // 2
    frequency = rope_base ** (-2.0 * jnp.arange(half_width, dtype=jnp.float32) / head_width)
    angles = jnp.arange(seq_len, dtype=jnp.float32)[:, None] * frequency[None, :]
    rotary_cosines = jnp.concatenate([jnp.cos(angles), jnp.cos(angles)], axis=1)
    rotary_sines = jnp.concatenate([jnp.sin(angles), jnp.sin(angles)], axis=1)
    return (rotary_cosines, rotary_sines)


def apply_rotary(tensor_in, rotary_cosines, rotary_sines):
    half_width = tensor_in.shape[-1] // 2
    turned = jnp.concatenate([-tensor_in[..., half_width:], tensor_in[..., :half_width]], axis=-1)
    return tensor_in * rotary_cosines[:, None, :] + turned * rotary_sines[:, None, :]


def unrotate(gradient, rotary_cosines, rotary_sines):
    half_width = gradient.shape[-1] // 2
    scaled = gradient * rotary_sines[:, None, :]
    rotated_back = jnp.concatenate([scaled[..., half_width:], -scaled[..., :half_width]], axis=-1)
    return gradient * rotary_cosines[:, None, :] + rotated_back


def attention_grads(example):
    query_per_head, key_heads, value_per_head, grad_out, seq_length = example
    seq_len = query_per_head.shape[0]
    inv_root = query_per_head.shape[-1] ** (-0.5)
    scores = (
        jnp.einsum("qhc,khc->hqk", query_per_head, key_heads, preferred_element_type=jnp.float32)
        * inv_root
    )
    query_pos = jnp.arange(seq_len, dtype=jnp.int32)[:, None]
    key_pos = jnp.arange(seq_len, dtype=jnp.int32)[None, :]
    allowed = (key_pos <= query_pos) & (key_pos < seq_length)
    scores = jnp.where(allowed[None], scores, masked_score)
    row_max = jnp.max(scores, axis=-1, keepdims=True)
    expon = jnp.exp(scores - row_max)
    attention = expon / jnp.sum(expon, axis=-1, keepdims=True)
    attention_low = attention.astype(jnp.bfloat16)
    grad_values = jnp.einsum(
        "hqk,qhc->khc", attention_low, grad_out, preferred_element_type=jnp.float32
    )
    grad_attention = jnp.einsum(
        "qhc,khc->hqk", grad_out, value_per_head, preferred_element_type=jnp.float32
    )
    inner_sum = jnp.sum(attention * grad_attention, axis=-1, keepdims=True)
    grad_scores = (attention * (grad_attention - inner_sum)).astype(jnp.bfloat16)
    grad_query = (
        jnp.einsum("hqk,khc->qhc", grad_scores, key_heads, preferred_element_type=jnp.float32)
        * inv_root
    )
    return (grad_query, grad_values)


def body(
    hidden,
    query_projection_matrix,
    key_projection_matrix,
    value_projection_matrix,
    adapter_down_maps,
    adapter_up_maps,
    cotangent,
    lengths,
    random_signs_down,
    random_signs_up,
):
    seq_count, seq_len, model_width = hidden.shape
    local_cols = query_projection_matrix.shape[1]
    heads_local = local_cols // HEAD_DIM
    token_matrix = hidden.reshape(seq_count * seq_len, model_width)

    def add_rows(weight_piece):
        return jnp.dot(token_matrix, weight_piece, preferred_element_type=jnp.float32)

    plain_query = add_rows(lax.all_gather(query_projection_matrix, "dp", axis=0, tiled=True))
    base_key = add_rows(lax.all_gather(key_projection_matrix, "dp", axis=0, tiled=True))
    plain_value = add_rows(lax.all_gather(value_projection_matrix, "dp", axis=0, tiled=True))
    rotary_cosines, rotary_sines = rope_tables(seq_len, HEAD_DIM)
    inner_hidden = jnp.einsum(
        "no,wio->nwi", token_matrix, adapter_down_maps, preferred_element_type=jnp.float32
    ).astype(jnp.bfloat16)
    raised_features = jnp.einsum(
        "kdg,dgj->kdj", inner_hidden, adapter_up_maps, preferred_element_type=jnp.float32
    )
    head_layout = (seq_count, seq_len, heads_local, HEAD_DIM)
    query_per_head = apply_rotary(
        (plain_query + adapter_scale * raised_features[:, 0]).reshape(head_layout),
        rotary_cosines,
        rotary_sines,
    ).astype(jnp.bfloat16)
    key_heads = apply_rotary(base_key.reshape(head_layout), rotary_cosines, rotary_sines).astype(
        jnp.bfloat16
    )
    value_per_head = (
        (plain_value + adapter_scale * raised_features[:, 1])
        .astype(jnp.bfloat16)
        .reshape(head_layout)
    )
    valid = jnp.arange(seq_len, dtype=jnp.int32)[None, :] < lengths[:, None]
    masked_out = jnp.where(valid[:, :, None], cotangent, jnp.zeros_like(cotangent)).reshape(
        head_layout
    )
    grad_query, grad_values = lax.map(
        attention_grads, (query_per_head, key_heads, value_per_head, masked_out, lengths)
    )
    grad_query = (
        unrotate(grad_query, rotary_cosines, rotary_sines)
        .astype(jnp.bfloat16)
        .reshape(seq_count, seq_len, local_cols)
    )
    grad_values = grad_values.astype(jnp.bfloat16).reshape(seq_count, seq_len, local_cols)
    per_head_gradient = jnp.stack([grad_query, grad_values], axis=2)
    branch_portion = jnp.einsum(
        "liov,ohv->lioh", per_head_gradient, adapter_up_maps, preferred_element_type=jnp.float32
    )
    adapter_branch = lax.psum(branch_portion, "tensor").astype(jnp.bfloat16)
    middle_seq = inner_hidden.reshape(seq_count, seq_len, 2, ADAPTER_RANK)
    up_map_gradient = adapter_scale * jnp.einsum(
        "esar,esac->earc", middle_seq, per_head_gradient, preferred_element_type=jnp.float32
    )
    parts_dp = lax.axis_size("dp")
    parts_tensor = lax.axis_size("tensor")
    row_block = model_width // (parts_dp * parts_tensor)
    hidden_blocks = hidden.reshape(seq_count, seq_len, parts_dp, parts_tensor, row_block)
    local_column_range = lax.dynamic_index_in_dim(
        hidden_blocks, lax.axis_index("tensor"), axis=3, keepdims=False
    )
    down_map_local = adapter_scale * jnp.einsum(
        "ykzu,ykhc->yhzuc", adapter_branch, local_column_range, preferred_element_type=jnp.float32
    )
    down_map_local = down_map_local.reshape(seq_count, parts_dp, 1, 2 * ADAPTER_RANK * row_block)
    slice_len = HEAD_DIM // parts_dp
    up_blocks = up_map_gradient.reshape(
        seq_count, 2, ADAPTER_RANK, heads_local, parts_dp, slice_len
    )
    up_blocks = up_blocks.transpose(0, 4, 1, 2, 3, 5).reshape(
        seq_count, parts_dp, 1, 2 * ADAPTER_RANK * heads_local * slice_len
    )
    packed = jnp.concatenate([down_map_local, up_blocks], axis=3).astype(jnp.bfloat16)
    routed = lax.all_to_all(packed, "dp", split_axis=1, concat_axis=0, tiled=True)
    gathered = routed.reshape(routed.shape[0], routed.shape[3])
    down_count = down_map_local.shape[3]
    down_table = random_signs_down.reshape(down_count, random_signs_down.shape[-1])
    up_table = random_signs_up.reshape(gathered.shape[1] - down_count, random_signs_up.shape[-1])
    own_rows = lax.psum_scatter(
        (
            jnp.dot(gathered[:, :down_count], down_table, preferred_element_type=jnp.float32)
            + jnp.dot(gathered[:, down_count:], up_table, preferred_element_type=jnp.float32)
        ).astype(jnp.bfloat16),
        "dp",
        scatter_dimension=0,
        tiled=True,
    )
    features_local = lax.psum_scatter(own_rows, "tensor", scatter_dimension=1, tiled=True).astype(
        jnp.float32
    )
    squares = lax.psum(jnp.sum(features_local * features_local, axis=1), "tensor")
    return features_local * lax.rsqrt(squares / FEAT + norm_eps)[:, None]


def solution(mesh):
    return jax.shard_map(
        body,
        mesh=mesh,
        in_specs=(
            P("dp", None, None),
            P("dp", "tensor"),
            P("dp", "tensor"),
            P("dp", "tensor"),
            P(),
            P(None, None, "tensor"),
            P("dp", None, "tensor"),
            P("dp"),
            P(None, None, ("dp", "tensor"), None),
            P(None, None, "tensor", "dp", None),
        ),
        out_specs=P("dp", "tensor"),
        check_vma=False,
    )
```

profile of v0, /device:TPU:1, one launch (start us, length us, event | category | flops | bytes accessed | tf_op | source)
XLA Modules:
  0.0 960.9 jit_solution(16384661594422788543)
XLA Ops:
  8.8 1.6 copy.57
  10.4 13.8 %copy.51 = bf16[2,512,5120]{1,2,0:T(8,128)(2,1)} copy(bf16[2,512,5120]{2,1,0:T(8,128)(2,1)} %param.12) | data formatting | bytes 20971520 | tf_op args[0]
  24.9 1.2 broadcast_select_fusion
  26.1 6.8 convolution_convert_fusion
  33.5 3.2 convolution_bitcast_fusion
  36.7 117.4 %all-gather.6.cloned.1.call-done = bf16[5120,640]{1,0:T(8,128)(2,1)} async-done(((bf16[160,640]{1,0:T(8,128)(2,1)}), bf16[5120,640]{1,0:T(8,128)(2,1)}) %all-gather.6.cloned.1.call-update) | async-done | bytes 6553616 | tf_op jit(solution)/shard_map/all_gather | solution.py:88
  154.2 13.3 %fusion.46 = f32[1024,640]{1,0:T(8,128)S(1)} fusion(f32[1024,2,640]{2,0,1:T(8,128)} %convolution_bitcast_fusion, bf16[1024,5120]{1,0:T(8,128)(2,1)} %bitcast.136, bf16[5120,640]{1,0:T(8,128)(2,1)} %all-gather.6.cloned.1.call-done), kind=kOutput, calls=%fused_computation.52 | convolution fusion | flops 6712197120 | bytes 22282240 | tf_op jit(solution)/shard_map/dot_general | solution.py:86
  167.5 2.3 reshape.164
  169.8 3.3 copy.54
  173.1 145.5 %all-gather.4.cloned.1.call-done = bf16[5120,640]{1,0:T(8,128)(2,1)} async-done(((bf16[160,640]{1,0:T(8,128)(2,1)}), bf16[5120,640]{1,0:T(8,128)(2,1)}) %all-gather.4.cloned.1.call-update) | async-done | bytes 6553616 | tf_op jit(solution)/shard_map/all_gather | solution.py:89
  318.6 9.6 copy.52
  328.1 1.9 slice_negate_fusion.1
  330.1 11.9 %fusion.39 = f32[2,512,5,128]{1,3,2,0:T(8,128)S(1)} fusion(bf16[5,128,5120,1]{2,1,0,3:T(8,128)(2,1)} %bitcast.140, bf16[2,512,5120]{2,1,0:T(8,128)(2,1)} %param.12), kind=kOutput, calls=%fused_computation.42 | convolution fusion | flops 6710886400 | bytes 19660800 | tf_op jit(solution)/shard_map/dot_general | solution.py:86
  341.9 1.5 copy-done.3
  343.4 1.8 slice_negate_fusion.2
  345.2 137.9 %all-gather.8.cloned.1.call-done = bf16[5120,640]{1,0:T(8,128)(2,1)} async-done(((bf16[160,640]{1,0:T(8,128)(2,1)}), bf16[5120,640]{1,0:T(8,128)(2,1)}) %all-gather.8.cloned.1.call-update) | async-done | bytes 6553616 | tf_op jit(solution)/shard_map/all_gather | solution.py:90
  483.1 14.2 %fusion.44 = bf16[1024,640]{1,0:T(8,128)(2,1)} fusion(f32[1024,2,640]{2,0,1:T(8,128)} %convolution_bitcast_fusion, bf16[1024,5120]{1,0:T(8,128)(2,1)} %bitcast.137, bf16[5120,640]{1,0:T(8,128)(2,1)} %all-gather.8.cloned.1.call-done), kind=kOutput, calls=%fused_computation.49 | convolution fusion | flops 6712852480 | bytes 20971520 | tf_op jit(solution)/shard_map/dot_general | solution.py:86
  497.3 4.1 reshape.160
  501.4 3.1 copy.62
  504.4 5.5 fusion.50
  509.9 22.3 %while.12 = (s32[]{:T(128)}, f32[2,512,5,128]{1,3,2,0:T(8,128)}, bf16[2,512,5,128]{1,3,2,0:T(8,128)(2,1)}, bf16[2,512,5,128]{1,3,2,0:T(8,128)(2,1)}, s32[2]{0:T(...) while((s32[]{:T(128)}, f32[2,512,5,128]{1,3,2,0:T(8,128)}, ...), condition=%wide.region_4.5_spmd, body=%wide.region_0.4_spmd.sunk | while | flops 1362688512 | bytes 75326712 | solution.py:116
  509.9 2.2 fusion.110
  513.5 2.5 fusion.112
  516.1 1.0 fusion.114
  517.4 0.9 multiply_reduce_fusion.2
  518.9 2.2 fusion.113
  521.1 2.2 fusion.110
  524.6 2.5 fusion.112
  527.2 1.0 fusion.114
  530.0 2.2 fusion.113
  532.2 2.1 broadcast_multiply_fusion
  534.6 2.5 fusion.51
  537.1 1.5 copy.63
  538.6 1.4 copy.64
  540.0 2.1 fusion.67
  542.1 34.5 %psum.14 = bf16[2,512,2,8]{1,3,2,0:T(8,128)(2,1)S(1)} all-reduce(f32[2,512,2,8]{1,3,2,0:T(8,128)S(1)} %fusion.67), channel_id=1, replica_groups=mesh['dp'=32,'tensor'=4] {'tensor'}, use_global_device_ids=true, to_apply=%region_5.6 | all-reduce | flops 16384 | bytes 98304 | tf_op jit(solution)/shard_map/psum | solution.py:129
  576.6 3.3 fusion.63
  582.4 6.6 all-to-all-start
  589.1 3.5 reshape.153
  592.6 3.8 all-to-all-done
  596.6 3.6 fusion.71
  600.1 1.5 fusion.41
  602.9 286.6 %all-reduce.3.cloned.1.call-done = bf16[64,4096]{1,0:T(8,128)(2,1)} async-done(((bf16[64,4096]{1,0:T(8,128)(2,1)}), bf16[64,4096]{1,0:T(8,128)(2,1)}) %all-reduce.3.cloned.1.call-update) | async-done | bytes 524304
  889.5 0.9 constant_dynamic-slice_fusion
  890.4 1.4 copy.79
  891.8 53.3 %reduce-scatter.4.cloned.1.call-done = bf16[1024,2]{1,0:T(8,128)(2,1)} async-done(((bf16[4096,2]{1,0:T(8,128)(2,1)}), bf16[1024,2]{1,0:T(8,128)(2,1)}) %reduce-scatter.4.cloned.1.call-update) | async-done | bytes 4112
  945.1 1.1 copy.80
  946.3 7.4 psum.15
  (81 shorter events, 13.3 us)
Async XLA Ops:
  6.5 19.5 %copy-start = (bf16[2,8,5120]{2,1,0:T(8,128)(2,1)S(1)}, bf16[2,8,5120]{2,1,0:T(8,128)(2,1)}, u32[]{:S(2)}) copy-start(bf16[2,8,5120]{2,1,0:T(8,128)(2,1)} %param.16) | copy-start | bytes 491524
  6.5 147.6 %all-gather.6.cloned.1.call-start = ((), (), s32[]{:S(2)}) async-start(), calls=%async_computation.3 | async-start | bytes 6758400 | tf_op jit(solution)/shard_map/all_gather | solution.py:88
  7.3 311.3 %all-gather.4.cloned.1.call-start = ((), (), s32[]{:S(2)}) async-start(), calls=%async_computation.2 | async-start | bytes 6758400 | tf_op jit(solution)/shard_map/all_gather | solution.py:89
  8.0 475.1 %all-gather.8.cloned.1.call-start = ((), (), s32[]{:S(2)}) async-start(), calls=%async_computation.4 | async-start | bytes 6758400 | tf_op jit(solution)/shard_map/all_gather | solution.py:90
  10.4 14.5 %copy-start.16 = (s32[2]{0:T(128)S(1)}, s32[2]{0:T(128)}, u32[]{:S(2)}) copy-start(s32[2]{0:T(128)} %param.19) | copy-start | bytes 28
  26.1 7.5 copy-start.14
  32.9 0.6 copy-start.12
  341.9 1.5 copy-start.3
  501.4 3.1 copy-start.4
  513.5 2.6 copy-start.5
  513.5 2.6 copy-start.11
  516.1 1.3 copy-start.8
  517.1 1.2 copy-start.6
  517.4 1.5 copy-start.2
  524.6 2.6 copy-start.5
  524.6 2.6 copy-start.11
  527.2 1.3 copy-start.8
  528.2 1.2 copy-start.6
  528.5 1.5 copy-start.2
  537.1 1.5 copy-start.7
  537.1 2.9 copy-start.15
  538.6 1.4 copy-start.9
  542.1 38.1 %copy-start.10 = (bf16[2,512,1,640]{3,1,2,0:T(8,128)(2,1)S(1)}, bf16[2,512,1,640]{3,1,2,0:T(8,128)(2,1)}, u32[]{:S(2)}) copy-start(bf16[2,512,1,640]{3,1,2,0:T(8,128)(2,1)} %copy.64) | copy-start | bytes 3932164
  542.1 38.1 %copy-start.13 = (bf16[1024,2,8]{0,2,1:T(8,128)(2,1)S(1)}, bf16[1024,2,8]{0,2,1:T(8,128)(2,1)}, u32[]{:S(2)}) copy-start(bf16[1024,2,8]{0,2,1:T(8,128)(2,1)} %copy-done.12) | copy-start | bytes 98308
  582.4 14.1 %all-to-all-start = ((bf16[2,32,1,960]{3,0,2,1:T(2,128)(2,1)}), bf16[2,32,1,960]{3,0,2,1:T(2,128)(2,1)S(1)}, u32[]{:S(2)}, u32[]{:S(2)}) async-start(bf16[2,32,1,960]{3,0,2,1:T(2,128)(2,1)} %pad_maximum_fusion.11), calls=%async_computation | async-start | bytes 262144 | tf_op jit(solution)/shard_map/all_to_all | solution.py:153
  589.1 300.5 %all-reduce.3.cloned.1.call-start = ((), (), s32[]{:S(2)}) async-start(), calls=%async_computation.6 | async-start | bytes 1048576
  596.5 357.8 %copy-start.1 = (bf16[2,8,5120]{2,1,0:T(8,128)(2,1)S(1)}, bf16[2,8,5120]{2,1,0:T(8,128)(2,1)}, u32[]{:S(2)}) copy-start(bf16[2,8,5120]{2,1,0:T(8,128)(2,1)} %param.16) | copy-start | bytes 491524
  600.1 1.6 copy-start.17
  601.6 343.4 %reduce-scatter.4.cloned.1.call-start = ((), (), s32[]{:S(2)}) async-start(), calls=%async_computation.5 | async-start | bytes 1310720
Sparse Core Ops, SparseCore 0:
  9.0 145.1 all-gather.5
  155.8 162.7 all-gather.3
  320.2 162.8 all-gather.7
  601.8 287.7 all-reduce.2
  892.0 53.0 reduce-scatter.3
where the time goes:
time: 962 us; the launch traced here: 961 us
  waiting for transfers between devices  747 us (78%)
  matrix products  72.7 us (8%)
  local copies, waits for them, and re-layouts  54.7 us (6%)
  blocking collectives  41.9 us (4%)
  other arithmetic  24.1 us (3%)
  between operations  14.1 us (1%)
    unnamed x7, waiting for transfers between devices  342 us
    all_gather x1, waiting for transfers between devices, body(): lax.all_gather(key_projection_matrix, 'dp', axis=0, tiled=True)  145 us
    all_gather x1, waiting for transfers between devices, body(): lax.all_gather(value_projection_matrix, 'dp', axis=0, tiled=True)  138 us
    all_gather x1, waiting for transfers between devices, body(): lax.all_gather(query_projection_matrix, 'dp', axis=0, tiled=True)  117 us
    dot_general x3, matrix products, add_rows(): jnp.dot(token_matrix, weight_piece, preferred_element_type=jnp.float32)  39.3 us
    psum x1, blocking collectives, body(): adapter_branch = lax.psum(branch_portion, 'tensor').astype(jnp.bfloat16)  34.5 us
    unnamed x32, local copies, waits for them, and re-layouts  21.5 us
  transfers between devices with their start and end apart: 6, of which 6 were waited for; matrix products, arithmetic and copies ran while one was open for 8% of the time, Pallas kernels for 0%

commit v1 on v0

--- a/solution.py
+++ b/solution.py
@@ -2,6 +2,7 @@
 import jax.numpy as jnp
 from jax import lax
 from jax.sharding import PartitionSpec as P
+from jax.lax import all_to_all, axis_size
 
 HEAD_DIM = 128
 ADAPTER_RANK = 8
@@ -77,6 +78,13 @@
     random_signs_down,
     random_signs_up,
 ):
+
+    def measure_teams(local_block):
+        row_out = axis_size("dp")
+        earlier = jnp.stack(row_out * [local_block])
+        mat_out = all_to_all(earlier, "dp", 0, 0)
+        return jnp.concatenate(mat_out, axis=0)
+
     seq_count, seq_len, model_width = hidden.shape
     local_cols = query_projection_matrix.shape[1]
     heads_local = local_cols // HEAD_DIM
@@ -85,7 +93,7 @@
     def add_rows(weight_piece):
         return jnp.dot(token_matrix, weight_piece, preferred_element_type=jnp.float32)
 
-    plain_query = add_rows(lax.all_gather(query_projection_matrix, "dp", axis=0, tiled=True))
+    plain_query = add_rows(measure_teams(query_projection_matrix))
     base_key = add_rows(lax.all_gather(key_projection_matrix, "dp", axis=0, tiled=True))
     plain_value = add_rows(lax.all_gather(value_projection_matrix, "dp", axis=0, tiled=True))
     rotary_cosines, rotary_sines = rope_tables(seq_len, HEAD_DIM)

time: 962 us -> 874 us (0.909)
  waiting for transfers between devices: 747 us -> 651 us
    all_gather x1 -> x0, waiting for transfers between devices: 117 us -> none  [body(): lax.all_gather(query_projection_matrix, 'dp', axis=0, tiled=True)]
    all_to_all x0 -> x1, waiting for transfers between devices: none -> 78.6 us  [measure_teams(): mat_out = all_to_all(earlier, 'dp', 0, 0)]
    all_gather x1, waiting for transfers between devices: 145 us -> 90 us  [body(): lax.all_gather(key_projection_matrix, 'dp', axis=0, tiled=True)]
    unnamed x7 -> x6, waiting for transfers between devices: 342 us -> 341 us
  transfers between devices with their start and end apart: 6 -> 6, of which waited for: 6 -> 6; matrix products, arithmetic and copies ran while one was open for 8% -> 9% of each run, Pallas kernels for 0% -> 0%
where the time goes in v1:
time: 874 us; the launch traced here: 872 us
  waiting for transfers between devices  651 us (74%)
  matrix products  73.6 us (8%)
  local copies, waits for them, and re-layouts  56.5 us (6%)
  blocking collectives  41.9 us (5%)
  other arithmetic  18.6 us (2%)
  starting transfers between devices  16.2 us (2%)
  between operations  14 us (2%)
    unnamed x6, waiting for transfers between devices  341 us
    all_gather x1, waiting for transfers between devices, body(): lax.all_gather(value_projection_matrix, 'dp', axis=0, tiled=True)  137 us
    all_gather x1, waiting for transfers between devices, body(): lax.all_gather(key_projection_matrix, 'dp', axis=0, tiled=True)  90 us
    all_to_all x1, waiting for transfers between devices, measure_teams(): mat_out = all_to_all(earlier, 'dp', 0, 0)  78.6 us
    dot_general x3, matrix products, add_rows(): jnp.dot(token_matrix, weight_piece, preferred_element_type=jnp.float32)  40.3 us
    psum x1, blocking collectives, body(): adapter_branch = lax.psum(branch_portion, 'tensor').astype(jnp.bfloat16)  34.5 us
    unnamed x32, local copies, waits for them, and re-layouts  19 us
  transfers between devices with their start and end apart: 6, of which 6 were waited for; matrix products, arithmetic and copies ran while one was open for 9% of the time, Pallas kernels for 0%

profile of v1, /device:TPU:1, one launch (start us, length us, event | category | flops | bytes accessed | tf_op | source)
XLA Modules:
  0.0 872.2 jit_solution(1019238752235554070)
XLA Ops:
  8.0 4.1 stack.4
  12.1 9.5 %all-to-all-start = ((bf16[32,160,640]{2,1,0:T(8,128)(2,1)}), bf16[32,160,640]{2,1,0:T(8,128)(2,1)}, u32[]{:S(2)}, u32[]{:S(2)}) async-start(bf16[32,160,640]{2,1,0:T(8,128)(2,1)} %stack.4), calls=%async_computation | async-start | bytes 13107200 | tf_op jit(solution)/shard_map/all_to_all | solution.py:85
  22.3 13.8 %copy.51 = bf16[2,512,5120]{1,2,0:T(8,128)(2,1)} copy(bf16[2,512,5120]{2,1,0:T(8,128)(2,1)} %param.12) | data formatting | bytes 20971520 | tf_op args[0]
  36.7 1.1 broadcast_select_fusion
  37.9 6.8 convolution_convert_fusion
  45.3 3.2 convolution_bitcast_fusion
  48.5 78.6 %all-to-all-done = bf16[32,160,640]{2,1,0:T(8,128)(2,1)} async-done(((bf16[32,160,640]{2,1,0:T(8,128)(2,1)}), bf16[32,160,640]{2,1,0:T(8,128)(2,1)}, u32[]{:S(2)}, u32[]{:S(2)}) %all-to-all-start) | async-done | bytes 6553632 | tf_op jit(solution)/shard_map/all_to_all | solution.py:85
  127.1 13.4 %fusion.46 = f32[1024,640]{1,0:T(8,128)S(1)} fusion(f32[1024,2,640]{2,0,1:T(8,128)} %convolution_bitcast_fusion, bf16[1024,5120]{1,0:T(8,128)(2,1)} %bitcast.137, bf16[5120,640]{1,0:T(8,128)(2,1)} %bitcast.19), kind=kOutput, calls=%fused_computation.52 | convolution fusion | flops 6712197120 | bytes 22282240 | tf_op jit(solution)/shard_map/dot_general | solution.py:94
  140.5 2.3 reshape.170
  142.8 3.3 copy.54
  146.2 90.0 %all-gather.3.cloned.1.call-done = bf16[5120,640]{1,0:T(8,128)(2,1)} async-done(((bf16[160,640]{1,0:T(8,128)(2,1)}), bf16[5120,640]{1,0:T(8,128)(2,1)}) %all-gather.3.cloned.1.call-update) | async-done | bytes 6553616 | tf_op jit(solution)/shard_map/all_gather | solution.py:97
  236.2 9.5 %copy.52 = bf16[640,5120]{1,0:T(8,128)(2,1)} copy(bf16[640,5120]{0,1:T(8,128)(2,1)} %bitcast.140) | data formatting | bytes 13107200 | tf_op jit(solution)/shard_map/dot_general | solution.py:94
  245.7 12.8 %fusion.39 = f32[2,512,5,128]{1,3,2,0:T(8,128)} fusion(bf16[5,128,5120,1]{2,1,0,3:T(8,128)(2,1)} %bitcast.141, bf16[2,512,5120]{2,1,0:T(8,128)(2,1)} %param.12), kind=kOutput, calls=%fused_computation.42 | convolution fusion | flops 6710886400 | bytes 19660800 | tf_op jit(solution)/shard_map/dot_general | solution.py:94
  258.5 137.5 %all-gather.5.cloned.1.call-done = bf16[5120,640]{1,0:T(8,128)(2,1)} async-done(((bf16[160,640]{1,0:T(8,128)(2,1)}), bf16[5120,640]{1,0:T(8,128)(2,1)}) %all-gather.5.cloned.1.call-update) | async-done | bytes 6553616 | tf_op jit(solution)/shard_map/all_gather | solution.py:98
  395.9 14.1 %fusion.44 = bf16[1024,640]{1,0:T(8,128)(2,1)} fusion(f32[1024,2,640]{2,0,1:T(8,128)} %convolution_bitcast_fusion, bf16[1024,5120]{1,0:T(8,128)(2,1)} %bitcast.138, bf16[5120,640]{1,0:T(8,128)(2,1)} %all-gather.5.cloned.1.call-done), kind=kOutput, calls=%fused_computation.49 | convolution fusion | flops 6712852480 | bytes 20971520 | tf_op jit(solution)/shard_map/dot_general | solution.py:94
  410.1 4.1 reshape.166
  414.1 3.1 copy.62
  417.2 0.8 slice_negate_fusion.1
  418.1 3.0 fusion.50
  421.0 22.2 %while.12 = (s32[]{:T(128)}, f32[2,512,5,128]{1,3,2,0:T(8,128)}, bf16[2,512,5,128]{1,3,2,0:T(8,128)(2,1)}, bf16[2,512,5,128]{1,3,2,0:T(8,128)(2,1)}, s32[2]{0:T(...) while((s32[]{:T(128)}, f32[2,512,5,128]{1,3,2,0:T(8,128)}, ...), condition=%wide.region_4.5_spmd, body=%wide.region_0.4_spmd.sunk | while | flops 1362688512 | bytes 75326712 | solution.py:124
  421.0 2.2 fusion.110
  424.6 2.5 fusion.112
  427.2 1.0 fusion.114
  428.5 0.9 multiply_reduce_fusion.2
  430.0 2.2 fusion.113
  432.2 2.2 fusion.110
  435.7 2.5 fusion.112
  438.3 1.0 fusion.114
  439.6 0.8 multiply_reduce_fusion.2
  441.1 2.2 fusion.113
  443.3 2.1 broadcast_multiply_fusion
  445.7 2.5 fusion.51
  448.2 1.7 copy.63
  449.9 1.4 copy.64
  451.3 2.1 fusion.67
  453.4 34.5 %psum.14 = bf16[2,512,2,8]{1,3,2,0:T(8,128)(2,1)S(1)} all-reduce(f32[2,512,2,8]{1,3,2,0:T(8,128)S(1)} %fusion.67), channel_id=1, replica_groups=mesh['dp'=32,'tensor'=4] {'tensor'}, use_global_device_ids=true, to_apply=%region_5.6 | all-reduce | flops 16384 | bytes 98304 | tf_op jit(solution)/shard_map/psum | solution.py:137
  487.9 3.3 fusion.63
  493.7 6.6 all-to-all-start.1
  500.4 3.5 reshape.159
  504.0 3.8 all-to-all-done.1
  507.9 3.6 fusion.71
  511.5 1.5 fusion.41
  514.3 286.6 %all-reduce.3.cloned.1.call-done = bf16[64,4096]{1,0:T(8,128)(2,1)} async-done(((bf16[64,4096]{1,0:T(8,128)(2,1)}), bf16[64,4096]{1,0:T(8,128)(2,1)}) %all-reduce.3.cloned.1.call-update) | async-done | bytes 524304
  800.9 0.9 constant_dynamic-slice_fusion
  801.7 1.4 copy.79
  803.1 53.3 %reduce-scatter.4.cloned.1.call-done = bf16[1024,2]{1,0:T(8,128)(2,1)} async-done(((bf16[4096,2]{1,0:T(8,128)(2,1)}), bf16[1024,2]{1,0:T(8,128)(2,1)}) %reduce-scatter.4.cloned.1.call-update) | async-done | bytes 4112
  856.4 1.1 copy.80
  857.6 7.4 psum.15
  (80 shorter events, 12.4 us)
Async XLA Ops:
  6.5 31.3 %copy-start = (bf16[2,8,5120]{2,1,0:T(8,128)(2,1)S(1)}, bf16[2,8,5120]{2,1,0:T(8,128)(2,1)}, u32[]{:S(2)}) copy-start(bf16[2,8,5120]{2,1,0:T(8,128)(2,1)} %param.16) | copy-start | bytes 491524
  6.5 229.6 %all-gather.3.cloned.1.call-start = ((), (), s32[]{:S(2)}) async-start(), calls=%async_computation.3 | async-start | bytes 6758400 | tf_op jit(solution)/shard_map/all_gather | solution.py:97
  7.3 388.7 %all-gather.5.cloned.1.call-start = ((), (), s32[]{:S(2)}) async-start(), calls=%async_computation.4 | async-start | bytes 6758400 | tf_op jit(solution)/shard_map/all_gather | solution.py:98
  12.1 9.5 %copy-start.4 = (bf16[2,512,640]{2,1,0:T(8,128)(2,1)S(1)}, bf16[2,512,640]{2,1,0:T(8,128)(2,1)}, u32[]{:S(2)}) copy-start(bf16[2,512,640]{2,1,0:T(8,128)(2,1)} %param.18) | copy-start | bytes 3932164
  12.1 115.0 %all-to-all-start = ((bf16[32,160,640]{2,1,0:T(8,128)(2,1)}), bf16[32,160,640]{2,1,0:T(8,128)(2,1)}, u32[]{:S(2)}, u32[]{:S(2)}) async-start(bf16[32,160,640]{2,1,0:T(8,128)(2,1)} %stack.4), calls=%async_computation | async-start | bytes 13107200 | tf_op jit(solution)/shard_map/all_to_all | solution.py:85
  22.3 14.4 %copy-start.16 = (s32[2]{0:T(128)S(1)}, s32[2]{0:T(128)}, u32[]{:S(2)}) copy-start(s32[2]{0:T(128)} %param.19) | copy-start | bytes 28
  37.9 7.4 copy-start.14
  44.7 0.6 copy-start.12
  414.1 3.1 copy-start.3
  424.6 2.6 copy-start.5
  424.6 2.6 copy-start.11
  427.2 1.3 copy-start.8
  428.2 1.2 copy-start.6
  428.5 1.5 copy-start.2
  435.7 2.6 copy-start.5
  435.7 2.6 copy-start.11
  438.3 1.3 copy-start.8
  439.3 1.2 copy-start.6
  439.6 1.5 copy-start.2
  448.1 1.7 copy-start.7
  448.1 3.2 copy-start.15
  449.9 1.4 copy-start.9
  453.4 38.1 %copy-start.10 = (bf16[2,512,1,640]{3,1,2,0:T(8,128)(2,1)S(1)}, bf16[2,512,1,640]{3,1,2,0:T(8,128)(2,1)}, u32[]{:S(2)}) copy-start(bf16[2,512,1,640]{3,1,2,0:T(8,128)(2,1)} %copy.64) | copy-start | bytes 3932164
  453.4 38.1 %copy-start.13 = (bf16[1024,2,8]{0,2,1:T(8,128)(2,1)S(1)}, bf16[1024,2,8]{0,2,1:T(8,128)(2,1)}, u32[]{:S(2)}) copy-start(bf16[1024,2,8]{0,2,1:T(8,128)(2,1)} %copy-done.12) | copy-start | bytes 98308
  493.7 14.1 %all-to-all-start.1 = ((bf16[2,32,1,960]{3,0,2,1:T(2,128)(2,1)}), bf16[2,32,1,960]{3,0,2,1:T(2,128)(2,1)S(1)}, u32[]{:S(2)}, u32[]{:S(2)}) async-start(bf16[2,32,1,960]{3,0,2,1:T(2,128)(2,1)} %pad_maximum_fusion.11), calls=%async_computation.1 | async-start | bytes 262144 | tf_op jit(solution)/shard_map/all_to_all | solution.py:161
  500.4 300.5 %all-reduce.3.cloned.1.call-start = ((), (), s32[]{:S(2)}) async-start(), calls=%async_computation.6 | async-start | bytes 1048576
  507.9 357.8 %copy-start.1 = (bf16[2,8,5120]{2,1,0:T(8,128)(2,1)S(1)}, bf16[2,8,5120]{2,1,0:T(8,128)(2,1)}, u32[]{:S(2)}) copy-start(bf16[2,8,5120]{2,1,0:T(8,128)(2,1)} %param.16) | copy-start | bytes 491524
  511.5 1.6 copy-start.17
  513.0 343.4 %reduce-scatter.4.cloned.1.call-start = ((), (), s32[]{:S(2)}) async-start(), calls=%async_computation.5 | async-start | bytes 1310720
Sparse Core Ops, SparseCore 0:
  9.0 227.1 all-gather.2
  237.8 158.0 all-gather.4
  513.1 287.7 all-reduce.2
  803.3 53.0 reduce-scatter.3
